TPU v7x, 32 devices: a whole 2x2x4 slice. The times are simulated.
32 devices in a mesh: seq: 16 (over z, y, core), dp: 2 (over x).
Axes of the slice: x: 2, y: 2, z: 4, core: 2. Of those that a mesh axis runs over, the one named last changes fastest.
Arguments:
- layer_input: bfloat16 [2, 2048, 4096], P('dp', 'seq'), may hold values from -0.3125 to 0.3125
- scan_input: bfloat16 [2, 2048, 2048], P('dp', 'seq'), may hold values from -6 to 6
- readout: bfloat16 [2, 2048, 64], P('dp', 'seq'), may hold values from -6 to 6
- log_decay: float32 [2, 2048, 32], P('dp', 'seq'), may hold values from -1 to 0
- output_cotangent: bfloat16 [2, 2048, 2048], P('dp', 'seq'), may hold values from -0.0078125 to 0.0078125
- write_weight: float32 [4096, 64], P('dp'), may hold values from -6 to 6
- first_moment: float32 [4096, 64], P('dp'), may hold values from -6 to 6
- second_moment: float32 [4096, 64], P('dp'), may hold values from 1 to 25
Outputs:
- decay_gradient: float32 [2, 2048, 32], P('dp', 'seq')
- new_weight: float32 [4096, 64], P('dp')
- new_first: float32 [4096, 64], P('dp')
- new_second: float32 [4096, 64], P('dp')
All inputs are finite; a program needn't handle non-finite values.
Results may differ from a plain program's by a relative error of at most 0.0039.
Values may be sent and summed in bfloat16 or wider, within the bound.
A program may use at most 64 MiB of HBM per device.

v0:
```python
import jax
import jax.numpy as jnp
from jax import lax
from jax.sharding import PartitionSpec as P

HALF_HEAD_COUNT = 32
HEAD_DIM = 64
STATE = 64
beta_one = 0.9
beta_two = 0.999
adam_count = 10.0
learn_rate = 0.01
weight_decay = 0.1
epsilon = 1e-08
highest = lax.Precision.HIGHEST


def entering(part, axis, combine, identity, reverse):
    count = lax.axis_size(axis)
    place = lax.axis_index(axis)
    ahead = count - 1 - place if reverse else place
    gathered = jax.tree.map(lambda a: lax.all_gather(a, axis), part)
    state = jax.tree.map(lambda a, e: jnp.zeros_like(a) + jnp.asarray(e, a.dtype), part, identity)

    def one(lap, state):
        source = count - 1 - lap if reverse else lap
        return combine(
            state, jax.tree.map(lambda a: lax.dynamic_index_in_dim(a, source, 0, False), gathered)
        )

    return lax.fori_loop(0, ahead, one, state)


def pair_combine(earlier_pair, later_pair):
    return (
        earlier_pair[0] * later_pair[0],
        later_pair[0][:, None, None] * earlier_pair[1] + later_pair[1],
    )


def adam_update(grad_rows, weight_rows, first_rows, second_rows):
    new_first = beta_one * first_rows + (1.0 - beta_one) * grad_rows
    new_second = beta_two * second_rows + (1.0 - beta_two) * grad_rows * grad_rows
    first_hat = new_first / (1.0 - beta_one**adam_count)
    second_hat = new_second / (1.0 - beta_two**adam_count)
    new_weight = weight_rows - learn_rate * (
        first_hat / (jnp.sqrt(second_hat) + epsilon) + weight_decay * weight_rows
    )
    return (new_weight, new_first, new_second)


def on_device(
    layer_input,
    scan_input,
    readout,
    log_decay,
    output_cotangent,
    write_weight,
    first_moment,
    second_moment,
):
    input_rows = layer_input[0]
    scan_rows = scan_input[0]
    read_rows = readout[0]
    decay_rows = log_decay[0]
    back_rows = output_cotangent[0]
    length = input_rows.shape[0]
    weight_half = write_weight.astype(jnp.bfloat16)
    write_sum = jnp.dot(
        input_rows,
        lax.all_gather(weight_half, "dp", axis=0, tiled=True),
        preferred_element_type=jnp.float32,
    )
    write_half = write_sum.astype(jnp.bfloat16)
    write_float = lax.optimization_barrier(write_half).astype(jnp.float32)
    running = jnp.cumsum(decay_rows, axis=0)
    overall = running[-1]
    to_end = jnp.exp(overall[None, :] - running)
    from_start = jnp.exp(running)
    scan_split = scan_rows.reshape(length, HALF_HEAD_COUNT, HEAD_DIM)
    back_split = back_rows.reshape(length, HALF_HEAD_COUNT, HEAD_DIM)
    scan_heads = scan_split.astype(jnp.float32)
    back_heads = back_split.astype(jnp.float32)
    read_float = read_rows.astype(jnp.float32)
    state_local = jnp.einsum(
        "shp,sn->hpn", scan_heads * to_end[:, :, None], write_float, precision=highest
    )
    reverse_local = jnp.einsum(
        "shp,sn->hpn", back_heads * from_start[:, :, None], read_float, precision=highest
    )
    decay_total = jnp.exp(overall)
    identity = (
        jnp.ones((HALF_HEAD_COUNT,), jnp.float32),
        jnp.zeros((HALF_HEAD_COUNT, HEAD_DIM, STATE), jnp.float32),
    )
    state_pair = entering((decay_total, state_local), "seq", pair_combine, identity, False)
    grad_pair = entering((decay_total, reverse_local), "seq", pair_combine, identity, True)
    state_before = state_pair[1]
    grad_after = grad_pair[1]
    term_one = decay_total * jnp.sum(grad_after * state_before, axis=(1, 2))
    grad_write = jnp.einsum("hpn,sn->shp", grad_after, write_float, precision=highest)
    second_rows = to_end * jnp.sum(scan_heads * grad_write, axis=2)
    term_two = jnp.cumsum(second_rows, axis=0) - second_rows
    state_read = jnp.einsum("hpn,sn->shp", state_before, read_float, precision=highest)
    third_rows = from_start * jnp.sum(back_heads * state_read, axis=2)
    term_three = jnp.flip(jnp.cumsum(jnp.flip(third_rows, 0), axis=0), 0)
    crossed = jnp.einsum("thp,shp->hts", scan_split, back_split, preferred_element_type=jnp.float32)
    heads_running = running.T
    spread = heads_running[:, None, :] - heads_running[:, :, None]
    row_index = lax.broadcasted_iota(jnp.int32, (length, length), 0)
    col_index = lax.broadcasted_iota(jnp.int32, (length, length), 1)
    kernel_mat = (
        jnp.where((row_index <= col_index)[None], jnp.exp(jnp.minimum(spread, 0.0)), 0.0) * crossed
    )
    write_read = jnp.dot(write_half, read_rows.T, preferred_element_type=jnp.float32)
    pairing = jnp.where((row_index < col_index)[None], kernel_mat * write_read[None], 0.0)
    balance = (jnp.sum(pairing, axis=2) - jnp.sum(pairing, axis=1)).T
    term_four = jnp.cumsum(balance, axis=0) - balance
    decay_grad = term_one[None, :] + term_two + term_three + term_four
    scaled_scan = (scan_heads * to_end[:, :, None]).reshape(length, HALF_HEAD_COUNT * HEAD_DIM)
    write_grad = jnp.dot(
        scaled_scan, grad_after.reshape(HALF_HEAD_COUNT * HEAD_DIM, STATE), precision=highest
    )
    write_grad = write_grad + jnp.dot(jnp.sum(kernel_mat, axis=0), read_float, precision=highest)
    grad_half = write_grad.astype(jnp.bfloat16)
    partial_grad = jnp.dot(input_rows.T, grad_half, preferred_element_type=jnp.float32)
    owner_grad = lax.psum_scatter(partial_grad, "dp", scatter_dimension=0, tiled=True)
    grad_rows = lax.psum(owner_grad, "seq")
    new_weight, new_first, new_second = adam_update(
        grad_rows, write_weight, first_moment, second_moment
    )
    return (decay_grad[None], new_weight, new_first, new_second)


def solution(mesh):
    in_specs = (
        P("dp", "seq", None),
        P("dp", "seq", None),
        P("dp", "seq", None),
        P("dp", "seq", None),
        P("dp", "seq", None),
        P("dp", None),
        P("dp", None),
        P("dp", None),
    )
    out_specs = (P("dp", "seq", None), P("dp", None), P("dp", None), P("dp", None))
    return jax.shard_map(
        on_device, mesh=mesh, in_specs=in_specs, out_specs=out_specs, check_vma=False
    )
```

profile of v0, /device:TPU:29, one launch (start us, length us, event | category | flops | bytes accessed | tf_op | source)
XLA Modules:
  0.0 436.1 jit_solution(12412782208266294412)
XLA Ops:
  7.2 0.9 copy.43
  8.1 0.2 reduce_window_sum.22
  8.4 1.3 copy.44
  9.8 1.6 fusion.17
  11.6 0.3 copy.46
  11.9 7.8 %all_gather.24 = bf16[4096,64]{0,1:T(8,128)(2,1)S(1)} all-gather(bf16[2048,64]{0,1:T(8,128)(2,1)S(1)} %convert_element_type.22), channel_id=1, replica_groups=mesh['seq'=16,'dp'=2] {'dp'}, dimensions={0}, use_global_device_ids=true | all-gather | bytes 786432 | tf_op jit(solution)/shard_map/all_gather | solution.py:71
  19.8 0.5 convolution_convert_fusion
  20.3 18.4 %all-gather.2 = f32[16,1,32]{2,1,0:T(1,128)S(1)} all-gather(f32[1,1,32]{2,1,0:T(1,128)S(1)} %get-tuple-element.175), channel_id=1, replica_groups=mesh['seq'=16,'dp'=2] {'seq'}, dimensions={0}, use_global_device_ids=true | all-gather | bytes 2176 | tf_op jit(solution)/shard_map/all_gather | solution.py:22
  38.7 0.2 fusion.20
  38.9 1.8 fusion
  40.8 95.8 %all-gather.6.cloned.1.call-done = f32[512,64,64]{2,1,0:T(8,128)} async-done(((f32[32,64,64]{2,1,0:T(8,128)}), f32[512,64,64]{2,1,0:T(8,128)}) %all-gather.6.cloned.1.call-update) | async-done | bytes 8388624 | tf_op jit(solution)/shard_map/all_gather | solution.py:22
  136.6 0.1 broadcast_in_dim.36.clone
  136.7 0.6 fusion.5
  137.4 1.9 fusion.7
  139.3 0.2 fusion.8
  139.5 1.3 convolution_bitcast_fusion
  140.9 42.5 %reduce-scatter.2.cloned.1.call-done = f32[2048,64]{0,1:T(8,128)} async-done(((f32[4096,64]{0,1:T(8,128)}), f32[2048,64]{0,1:T(8,128)}) %reduce-scatter.2.cloned.1.call-update) | async-done | bytes 524304 | tf_op jit(solution)/shard_map/reduce_scatter | solution.py:127
  183.4 1.6 fusion.4
  185.1 0.1 copy.55
  185.2 0.2 reduce_window_sum.32
  185.4 0.1 copy.48
  185.5 0.2 reduce_window_sum.23
  185.8 90.6 %all-reduce.2.cloned.1.call-done = f32[2048,64]{0,1:T(8,128)} async-done(((f32[2048,64]{0,1:T(8,128)}), f32[2048,64]{0,1:T(8,128)}) %all-reduce.2.cloned.1.call-update) | async-done | bytes 524304 | tf_op jit(solution)/shard_map/psum | solution.py:128
  276.4 2.7 multiply_subtract_fusion
  279.2 125.0 %all-gather.8.cloned.1.call-done = f32[512,64,64]{2,1,0:T(8,128)} async-done(((f32[32,64,64]{2,1,0:T(8,128)}), f32[512,64,64]{2,1,0:T(8,128)}) %all-gather.8.cloned.1.call-update) | async-done | bytes 8388624 | tf_op jit(solution)/shard_map/all_gather | solution.py:22
  404.2 0.1 broadcast_in_dim.36
  404.3 22.4 %while.27 = (s32[]{:T(128)}, f32[32,64,64]{2,1,0:T(8,128)S(1)}, s32[]{:T(128)}, f32[16,32]{1,0:T(8,128)S(1)}, f32[16,32,64,64]{3,2,1,0:T(8,128)}, /*index=5*/s32[]{:T(128)}, s32[]{:T(128)}, s32[]{:T(128)}) while((s32[]{:T(128)}, f32[32,64,64]{2,1,0:T(8,128)S(1)}, s32[]{:T(128)}, f32[16,32]{1,0:T(8,128)S(1)}, f32[16,32,64,64]{3,2,1,0:T(8,128)}, ...), condition=%wide.region_4.5_spmd, body=%wide.region_3.4_spmd.sunk | while | flops 262149 | bytes 1573375 | solution.py:31
  404.3 1.4 bitcast_add_fusion.5
  405.8 1.4 bitcast_add_fusion.5
  407.3 1.4 bitcast_add_fusion.5
  408.8 1.4 bitcast_add_fusion.5
  410.3 1.4 bitcast_add_fusion.5
  411.8 1.4 bitcast_add_fusion.5
  413.3 1.4 bitcast_add_fusion.5
  414.8 1.4 bitcast_add_fusion.5
  416.3 1.4 bitcast_add_fusion.5
  417.8 1.4 bitcast_add_fusion.5
  419.3 1.4 bitcast_add_fusion.5
  420.8 1.4 bitcast_add_fusion.5
  422.3 1.4 bitcast_add_fusion.5
  423.8 1.4 bitcast_add_fusion.5
  425.3 1.4 bitcast_add_fusion.5
  426.8 0.3 multiply_reduce_fusion
  427.1 0.7 copy-done.2
  427.8 0.6 fusion.6
  428.5 0.1 copy.51
  428.6 0.2 reduce_window_sum.27
  428.9 0.7 add_bitcast_fusion
  (52 shorter events, 1.1 us)
Async XLA Ops:
  7.2 12.6 %copy-start = (bf16[1,128,4096]{2,1,0:T(8,128)(2,1)S(1)}, bf16[1,128,4096]{2,1,0:T(8,128)(2,1)}, u32[]{:S(2)}) copy-start(bf16[1,128,4096]{2,1,0:T(8,128)(2,1)} %param.12) | copy-start | bytes 3145732
  7.2 2.6 copy-start.5
  7.2 129.4 %all-gather.6.cloned.1.call-start = ((), (), s32[]{:S(2)}) async-start(), calls=%async_computation.3 | async-start | bytes 17825792 | tf_op jit(solution)/shard_map/all_gather | solution.py:22
  9.7 29.2 %copy-start.1 = (bf16[1,128,2048]{1,2,0:T(8,128)(2,1)}, bf16[1,128,2048]{1,2,0:T(8,128)(2,1)S(1)}, u32[]{:S(2)}) copy-start(bf16[1,128,2048]{1,2,0:T(8,128)(2,1)S(1)} %copy.44) | copy-start | bytes 1572868
  9.7 1.9 copy-start.4
  9.8 2.0 copy-start.3
  11.5 171.9 %reduce-scatter.2.cloned.1.call-start = ((), (), s32[]{:S(2)}) async-start(), calls=%async_computation.1 | async-start | bytes 1572864 | tf_op jit(solution)/shard_map/reduce_scatter | solution.py:127
  140.8 135.6 %all-reduce.2.cloned.1.call-start = ((), (), s32[]{:S(2)}) async-start(), calls=%async_computation.2 | async-start | bytes 1048576 | tf_op jit(solution)/shard_map/psum | solution.py:128
  183.4 220.8 %all-gather.8.cloned.1.call-start = ((), (), s32[]{:S(2)}) async-start(), calls=%async_computation.4 | async-start | bytes 17825792 | tf_op jit(solution)/shard_map/all_gather | solution.py:22
  426.8 1.0 copy-start.2
Sparse Core Ops, SparseCore 0:
  11.6 124.9 all-gather.5
  140.9 42.3 reduce-scatter.1
  186.8 89.6 all-reduce.1
  278.4 125.7 all-gather.7
where the time goes:
time: 437 us; the launch traced here: 436 us
  waiting for transfers between devices  354 us (81%)
  other arithmetic  26.4 us (6%)
  blocking collectives  26.2 us (6%)
  between operations  14 us (3%)
  matrix products  10.4 us (2%)
    all_gather x2, waiting for transfers between devices, entering(): gathered = jax.tree.map(lambda a: lax.all_gather(a, axis), part)  221 us
    psum x1, waiting for transfers between devices, on_device(): grad_rows = lax.psum(owner_grad, 'seq')  90.6 us
    reduce_scatter x1, waiting for transfers between devices, on_device(): lax.psum_scatter(partial_grad, 'dp', scatter_dimension=0, tiled=True)  42.5 us
    add x15, other arithmetic, pair_combine(): later_pair[0][:, None, None] * earlier_pair[1] + later_pair[1]  21.7 us
    all_gather x1, blocking collectives, entering(): gathered = jax.tree.map(lambda a: lax.all_gather(a, axis), part)  18.4 us
  transfers between devices with their start and end apart: 4, of which 4 were waited for; matrix products, arithmetic and copies ran while one was open for 2% of the time, Pallas kernels for 0%

commit v1 on v0

--- a/solution.py
+++ b/solution.py
@@ -125,7 +125,11 @@
     grad_half = write_grad.astype(jnp.bfloat16)
     partial_grad = jnp.dot(input_rows.T, grad_half, preferred_element_type=jnp.float32)
     owner_grad = lax.psum_scatter(partial_grad, "dp", scatter_dimension=0, tiled=True)
-    grad_rows = lax.psum(owner_grad, "seq")
+    grad_rows = owner_grad
+    for hop in (1, 2, 4, 8):
+        grad_rows = grad_rows + lax.ppermute(
+            grad_rows, "seq", [(dev, dev ^ hop) for dev in range(16)]
+        )
     new_weight, new_first, new_second = adam_update(
         grad_rows, write_weight, first_moment, second_moment
     )

time: 437 us -> 370 us (0.85)
  waiting for transfers between devices: 354 us -> 284 us
    ppermute x0 -> x4, waiting for transfers between devices: none -> 113 us  [on_device(): lax.ppermute(grad_rows, 'seq', [(dev, dev ^ hop) for dev in range(16)])]
    all_gather x2, waiting for transfers between devices: 221 us -> 130 us  [entering(): gathered = jax.tree.map(lambda a: lax.all_gather(a, axis), part)]
    psum x1 -> x0, waiting for transfers between devices: 90.6 us -> none  [on_device(): grad_rows = lax.psum(owner_grad, 'seq')]
  transfers between devices with their start and end apart: 4 -> 7, of which waited for: 4 -> 7; matrix products, arithmetic and copies ran while one was open for 2% -> 3% of each run, Pallas kernels for 0% -> 0%
where the time goes in v1:
time: 370 us; the launch traced here: 369 us
  waiting for transfers between devices  284 us (77%)
  other arithmetic  27.7 us (7%)
  blocking collectives  26.2 us (7%)
  between operations  14 us (4%)
  matrix products  11.5 us (3%)
    all_gather x2, waiting for transfers between devices, entering(): gathered = jax.tree.map(lambda a: lax.all_gather(a, axis), part)  130 us
    ppermute x4, waiting for transfers between devices, on_device(): lax.ppermute(grad_rows, 'seq', [(dev, dev ^ hop) for dev in range(16)])  113 us
    reduce_scatter x1, waiting for transfers between devices, on_device(): lax.psum_scatter(partial_grad, 'dp', scatter_dimension=0, tiled=True)  40.7 us
    add x15, other arithmetic, pair_combine(): later_pair[0][:, None, None] * earlier_pair[1] + later_pair[1]  21.7 us
    all_gather x1, blocking collectives, entering(): gathered = jax.tree.map(lambda a: lax.all_gather(a, axis), part)  18.4 us
    all_gather x1, blocking collectives, on_device(): lax.all_gather(weight_half, 'dp', axis=0, tiled=True)  7.86 us
  transfers between devices with their start and end apart: 7, of which 7 were waited for; matrix products, arithmetic and copies ran while one was open for 3% of the time, Pallas kernels for 0%

profile of v1, /device:TPU:29, one launch (start us, length us, event | category | flops | bytes accessed | tf_op | source)
XLA Modules:
  0.0 368.8 jit_solution(12057582669305195632)
XLA Ops:
  7.2 1.4 copy.44
  8.6 0.8 copy.43
  9.5 0.2 reduce_window_sum.22
  9.8 1.6 fusion.17
  11.7 0.3 copy.46
  12.0 7.9 %all_gather.24 = bf16[4096,64]{0,1:T(8,128)(2,1)S(1)} all-gather(bf16[2048,64]{0,1:T(8,128)(2,1)S(1)} %convert_element_type.22), channel_id=1, replica_groups=mesh['seq'=16,'dp'=2] {'dp'}, dimensions={0}, use_global_device_ids=true | all-gather | bytes 786432 | tf_op jit(solution)/shard_map/all_gather | solution.py:71
  19.9 0.5 convolution_convert_fusion
  20.3 18.4 %all-gather.2 = f32[16,1,32]{2,1,0:T(1,128)S(1)} all-gather(f32[1,1,32]{2,1,0:T(1,128)S(1)} %get-tuple-element.175), channel_id=1, replica_groups=mesh['seq'=16,'dp'=2] {'seq'}, dimensions={0}, use_global_device_ids=true | all-gather | bytes 2176 | tf_op jit(solution)/shard_map/all_gather | solution.py:22
  38.7 0.2 fusion.20
  38.9 1.8 fusion
  40.8 95.8 %all-gather.6.cloned.1.call-done = f32[512,64,64]{2,1,0:T(8,128)} async-done(((f32[32,64,64]{2,1,0:T(8,128)}), f32[512,64,64]{2,1,0:T(8,128)}) %all-gather.6.cloned.1.call-update) | async-done | bytes 8388624 | tf_op jit(solution)/shard_map/all_gather | solution.py:22
  136.7 0.6 fusion.5
  137.4 1.9 fusion.7
  139.3 0.2 fusion.8
  139.5 1.3 convolution_bitcast_fusion
  140.9 1.6 fusion.4
  142.6 40.7 %reduce-scatter.2.cloned.1.call-done = f32[2048,64]{0,1:T(8,128)} async-done(((f32[4096,64]{0,1:T(8,128)}), f32[2048,64]{0,1:T(8,128)}) %reduce-scatter.2.cloned.1.call-update) | async-done | bytes 524304 | tf_op jit(solution)/shard_map/reduce_scatter | solution.py:127
  183.3 0.8 collective-permute-start
  184.2 1.7 collective-permute-done
  185.9 1.1 add.93
  187.0 0.3 collective-permute-start.1
  187.4 17.0 %collective-permute-done.1 = f32[2048,64]{0,1:T(8,128)S(1)} collective-permute-done((f32[2048,64]{0,1:T(8,128)S(1)}, f32[2048,64]{0,1:T(8,128)S(1)}, u32[]{:S(2)}, u32[]{:S(2)}) %collective-permute-start.1) | collective-permute-done | bytes 524320 | tf_op jit(solution)/shard_map/ppermute | solution.py:130
  204.4 0.4 collective-permute-start.2
  204.8 36.5 %collective-permute-done.2 = f32[2048,64]{0,1:T(8,128)S(1)} collective-permute-done((f32[2048,64]{0,1:T(8,128)S(1)}, f32[2048,64]{0,1:T(8,128)S(1)}, u32[]{:S(2)}, u32[]{:S(2)}) %collective-permute-start.2) | collective-permute-done | bytes 524320 | tf_op jit(solution)/shard_map/ppermute | solution.py:130
  241.8 0.2 reduce_window_sum.23
  242.1 58.0 %collective-permute-done.3 = f32[2048,64]{0,1:T(8,128)} collective-permute-done((f32[2048,64]{0,1:T(8,128)S(1)}, f32[2048,64]{0,1:T(8,128)}, u32[]{:S(2)}, u32[]{:S(2)}) %collective-permute-start.3) | collective-permute-done | bytes 524320 | tf_op jit(solution)/shard_map/ppermute | solution.py:130
  300.0 2.8 multiply_subtract_fusion
  302.8 33.8 %all-gather.8.cloned.1.call-done = f32[512,64,64]{2,1,0:T(8,128)} async-done(((f32[32,64,64]{2,1,0:T(8,128)}), f32[512,64,64]{2,1,0:T(8,128)}) %all-gather.8.cloned.1.call-update) | async-done | bytes 8388624 | tf_op jit(solution)/shard_map/all_gather | solution.py:22
  336.7 22.4 %while.27 = (s32[]{:T(128)}, f32[32,64,64]{2,1,0:T(8,128)S(1)}, s32[]{:T(128)}, f32[16,32]{1,0:T(8,128)S(1)}, f32[16,32,64,64]{3,2,1,0:T(8,128)}, /*index=5*/s32[]{:T(128)}, s32[]{:T(128)}, s32[]{:T(128)}) while((s32[]{:T(128)}, f32[32,64,64]{2,1,0:T(8,128)S(1)}, s32[]{:T(128)}, f32[16,32]{1,0:T(8,128)S(1)}, f32[16,32,64,64]{3,2,1,0:T(8,128)}, ...), condition=%wide.region_4.5_spmd, body=%wide.region_3.4_spmd.sunk | while | flops 262149 | bytes 1573383 | solution.py:31
  336.8 1.4 bitcast_add_fusion.5
  338.3 1.4 bitcast_add_fusion.5
  339.7 1.4 bitcast_add_fusion.5
  341.2 1.4 bitcast_add_fusion.5
  342.7 1.4 bitcast_add_fusion.5
  344.2 1.4 bitcast_add_fusion.5
  345.7 1.4 bitcast_add_fusion.5
  347.2 1.4 bitcast_add_fusion.5
  348.7 1.4 bitcast_add_fusion.5
  350.2 1.4 bitcast_add_fusion.5
  351.7 1.4 bitcast_add_fusion.5
  353.2 1.4 bitcast_add_fusion.5
  354.7 1.4 bitcast_add_fusion.5
  356.2 1.4 bitcast_add_fusion.5
  357.6 1.4 bitcast_add_fusion.5
  359.1 1.7 fusion.6
  360.8 0.3 multiply_reduce_fusion
  361.3 0.2 reduce_window_sum.27
  361.6 0.7 add_bitcast_fusion
  (58 shorter events, 2.0 us)
Async XLA Ops:
  7.2 12.7 %copy-start = (bf16[1,128,4096]{2,1,0:T(8,128)(2,1)S(1)}, bf16[1,128,4096]{2,1,0:T(8,128)(2,1)}, u32[]{:S(2)}) copy-start(bf16[1,128,4096]{2,1,0:T(8,128)(2,1)} %param.12) | copy-start | bytes 3145732
  7.2 2.7 copy-start.4
  7.2 129.4 %all-gather.6.cloned.1.call-start = ((), (), s32[]{:S(2)}) async-start(), calls=%async_computation.2 | async-start | bytes 17825792 | tf_op jit(solution)/shard_map/all_gather | solution.py:22
  8.6 30.3 %copy-start.1 = (bf16[1,128,2048]{1,2,0:T(8,128)(2,1)}, bf16[1,128,2048]{1,2,0:T(8,128)(2,1)S(1)}, u32[]{:S(2)}) copy-start(bf16[1,128,2048]{1,2,0:T(8,128)(2,1)S(1)} %copy.44) | copy-start | bytes 1572868
  9.7 1.9 copy-start.2
  9.8 1.8 copy-start.3
  11.5 171.9 %reduce-scatter.2.cloned.1.call-start = ((), (), s32[]{:S(2)}) async-start(), calls=%async_computation.1 | async-start | bytes 1572864 | tf_op jit(solution)/shard_map/reduce_scatter | solution.py:127
  140.9 195.7 %all-gather.8.cloned.1.call-start = ((), (), s32[]{:S(2)}) async-start(), calls=%async_computation.3 | async-start | bytes 17825792 | tf_op jit(solution)/shard_map/all_gather | solution.py:22
  183.3 2.6 collective-permute-start
  187.0 17.3 %collective-permute-start.1 = (f32[2048,64]{0,1:T(8,128)S(1)}, f32[2048,64]{0,1:T(8,128)S(1)}, u32[]{:S(2)}, u32[]{:S(2)}) collective-permute-start(f32[2048,64]{0,1:T(8,128)S(1)} %add.93), channel_id=1, source_target_pairs={{0,4},{2,6},{4,0},{6,2},{8,12},{10,14},{12,8},{14,10},{16,20},{18,... | collective-permute-start | bytes 1572872 | tf_op jit(solution)/shard_map/ppermute | solution.py:130
  204.4 36.8 %collective-permute-start.2 = (f32[2048,64]{0,1:T(8,128)S(1)}, f32[2048,64]{0,1:T(8,128)S(1)}, u32[]{:S(2)}, u32[]{:S(2)}) collective-permute-start(f32[2048,64]{0,1:T(8,128)S(1)} %add.94), channel_id=1, source_target_pairs={{0,8},{2,10},{4,12},{6,14},{8,0},{10,2},{12,4},{14,6},{16,24},{18,... | collective-permute-start | bytes 1572872 | tf_op jit(solution)/shard_map/ppermute | solution.py:130
  241.3 58.8 %collective-permute-start.3 = (f32[2048,64]{0,1:T(8,128)S(1)}, f32[2048,64]{0,1:T(8,128)}, u32[]{:S(2)}, u32[]{:S(2)}) collective-permute-start(f32[2048,64]{0,1:T(8,128)S(1)} %add.95), channel_id=1, source_target_pairs={{0,16},{2,18},{4,20},{6,22},{8,24},{10,26},{12,28},{14,30},{16,0},... | collective-permute-start | bytes 1572872 | tf_op jit(solution)/shard_map/ppermute | solution.py:130
Sparse Core Ops, SparseCore 0:
  11.6 124.9 all-gather.5
  141.0 42.2 reduce-scatter.1
  185.5 151.0 all-gather.7
